TPU v7x, 32 devices: a whole 2x2x4 slice. The times are simulated.
32 devices in a mesh: rep: 1, seq: 16 (over z, y, core), head: 2 (over x).
Axes of the slice: x: 2, y: 2, z: 4, core: 2. Of those that a mesh axis runs over, the one named last changes fastest.
Arguments:
- states: bfloat16 [256, 8192], P('rep', 'seq'), may hold values from -6 to 6
- w_query: bfloat16 [8192, 8192], P('seq', 'head'), may hold values from -0.0625 to 0.0625
- w_key: bfloat16 [8192, 1024], P('seq', 'head'), may hold values from -0.3125 to 0.3125
- w_value: bfloat16 [8192, 1024], P('seq', 'head'), may hold values from -0.25 to 0.25
- w_out: bfloat16 [8192, 8192], P('head', 'seq'), may hold values from -0.09375 to 0.09375
- key_cache: bfloat16 [2, 8192, 1024], P('rep', 'seq', 'head'), may hold values from -480 to 480
- value_cache: bfloat16 [2, 8192, 1024], P('rep', 'seq', 'head'), may hold values from -24 to 24
- parents: int32 [2, 128], P('rep'), may hold values from 0 to 126, as said below
- cache_lengths: int32 [2], P('rep'), may hold values from 2048 to 8192, as said below
Outputs:
- attended: bfloat16 [256, 8192], P('rep', ('seq', 'head'))
Inputs may be any that keep to these rules, and one draw needn't show every extreme that they name: parents[t, 0] = 0, parents[t, i] < i for i >= 1, and the last node's parent is node 126. `cache_lengths`: at least one sequence fills all 8192 positions.
All inputs are finite; a program needn't handle non-finite values.
Results may differ from a plain program's by a relative error of at most 0.014.
The roundings to bfloat16 on the way count: a program that leaves them out, or rounds other values in their place, can miss the bound.
Values may be sent and summed in bfloat16 or wider, within the bound.
No kernel may reach another device: no remote copies, remote signals or barrier semaphores. Data moves between devices by JAX's collectives and lax.ppermute only.
A program may use at most 320 MiB of HBM per device.

v0:
```python
import jax
import jax.numpy as jnp
from jax import lax
from jax.sharding import PartitionSpec as P

HEAD_DIM = 128
rope_base = 500000.0
neg_big = -1e30


def ancestry(parents):
    count = parents.shape[1]
    ident = jnp.eye(count, dtype=jnp.float32)
    onehot = (parents[:, :, None] == jnp.arange(count, dtype=jnp.int32)[None, None, :]).astype(
        jnp.float32
    )
    reach = jnp.minimum(ident[None] + onehot, 1.0)
    for level in range(max(1, (count - 1).bit_length())):
        reach = jnp.minimum(
            jnp.einsum("tij,tjk->tik", reach, reach, precision=lax.Precision.HIGHEST), 1.0
        )
    return reach


def rotate(values, position):
    count = values.shape[0]
    half = HEAD_DIM // 2
    shaped = values.reshape(count, -1, HEAD_DIM)
    freq = rope_base ** (-(jnp.arange(half, dtype=jnp.float32) * 2.0 / HEAD_DIM))
    angle = position[:, None] * freq[None, :]
    cosine = jnp.cos(angle)[:, None, :]
    sine = jnp.sin(angle)[:, None, :]
    first = shaped[..., :half]
    second = shaped[..., half:]
    turned = jnp.concatenate([first * cosine - second * sine, second * cosine + first * sine], -1)
    return turned.reshape(count, -1)


def combine(left, right):
    top = jnp.maximum(left[0], right[0])
    scale_left = jnp.exp(left[0] - top)
    scale_right = jnp.exp(right[0] - top)
    return (
        top,
        left[1] * scale_left + right[1] * scale_right,
        left[2] * scale_left[..., None] + right[2] * scale_right[..., None],
    )


def cache_state(query, keys, values, length, offset):
    total = keys.shape[0]
    block = min(total, 2048)
    count = total // block
    rows_here, kv_local, group, width = query.shape
    scale = width ** (-0.5)
    keys = keys.reshape(count, block, kv_local, width)
    values = values.reshape(count, block, kv_local, width)

    def step(carry, inputs):
        key_block, value_block, first = inputs
        valid = offset + first + jnp.arange(block, dtype=jnp.int32) < length
        scores = (
            jnp.einsum("rkgd,nkd->rkgn", query, key_block, preferred_element_type=jnp.float32)
            * scale
        )
        scores = jnp.where(valid, scores, neg_big)
        top = jnp.maximum(carry[0], jnp.max(scores, -1))
        weights = jnp.where(valid, jnp.exp(scores - top[..., None]), 0.0)
        shrink = jnp.exp(carry[0] - top)
        mass = carry[1] * shrink + jnp.sum(weights, -1)
        acc = carry[2] * shrink[..., None] + jnp.einsum(
            "rkgn,nkd->rkgd",
            weights.astype(jnp.bfloat16),
            value_block,
            preferred_element_type=jnp.float32,
        )
        return ((top, mass, acc), None)

    init = (
        jnp.full((rows_here, kv_local, group), neg_big, jnp.float32),
        jnp.zeros((rows_here, kv_local, group), jnp.float32),
        jnp.zeros((rows_here, kv_local, group, width), jnp.float32),
    )
    firsts = jnp.arange(count, dtype=jnp.int32) * block
    state, _ = lax.scan(step, init, (keys, values, firsts))
    return state


def tree_state(query, new_keys, new_values, allowed):
    rows_here, kv_local, group, width = query.shape
    scale = width ** (-0.5)
    keys = new_keys.reshape(-1, kv_local, width)
    values = new_values.reshape(-1, kv_local, width)
    mask = allowed[:, None, None, :]
    scores = jnp.einsum("rkgd,nkd->rkgn", query, keys, preferred_element_type=jnp.float32) * scale
    scores = jnp.where(mask, scores, neg_big)
    top = jnp.max(scores, -1)
    weights = jnp.where(mask, jnp.exp(scores - top[..., None]), 0.0)
    acc = jnp.einsum(
        "rkgn,nkd->rkgd", weights.astype(jnp.bfloat16), values, preferred_element_type=jnp.float32
    )
    return (top, jnp.sum(weights, -1), acc)


def local(states, w_query, w_key, w_value, w_out, key_cache, value_cache, parents, cache_lengths):
    trees, tree_rows = parents.shape
    rows = trees * tree_rows
    kv_local = key_cache.shape[2] // HEAD_DIM
    heads_local = w_query.shape[1] // HEAD_DIM
    group = heads_local // kv_local
    reach = ancestry(parents)
    position = (cache_lengths.astype(jnp.float32)[:, None] + jnp.sum(reach, -1) - 1.0).reshape(-1)
    allowed = (jnp.eye(trees, dtype=jnp.float32)[:, None, :, None] * reach[:, :, None, :]).reshape(
        rows, rows
    ) > 0.5
    q_part = jnp.dot(states, w_query, preferred_element_type=jnp.float32)
    k_part = jnp.dot(states, w_key, preferred_element_type=jnp.float32)
    v_part = jnp.dot(states, w_value, preferred_element_type=jnp.float32)
    q_raw, k_raw, v_raw = lax.psum((q_part, k_part, v_part), "seq")
    queries = rotate(q_raw, position).astype(jnp.bfloat16)
    new_keys = rotate(k_raw, position).astype(jnp.bfloat16)
    new_values = v_raw.astype(jnp.bfloat16)
    query_heads = queries.reshape(rows, kv_local, group, HEAD_DIM)
    offset = lax.axis_index("seq") * key_cache.shape[1]
    parts_list = []
    for tree in range(trees):
        parts_list.append(
            cache_state(
                query_heads[tree * tree_rows : (tree + 1) * tree_rows],
                key_cache[tree],
                value_cache[tree],
                cache_lengths[tree],
                offset,
            )
        )
    peak = jnp.concatenate([item[0] for item in parts_list], 0)
    mass = jnp.concatenate([item[1] for item in parts_list], 0)
    acc = jnp.concatenate([item[2] for item in parts_list], 0)
    summit = lax.pmax(peak, "seq")
    factor = jnp.exp(peak - summit)
    mass_share, acc_share = (
        lax.psum_scatter(mass * factor, "seq", scatter_dimension=0, tiled=True),
        lax.psum_scatter(acc * factor[..., None], "seq", scatter_dimension=0, tiled=True),
    )
    share = mass_share.shape[0]
    first_row = lax.axis_index("seq") * share
    summit_share = lax.dynamic_slice_in_dim(summit, first_row, share)
    query_share = lax.dynamic_slice_in_dim(query_heads, first_row, share)
    allowed_share = lax.dynamic_slice_in_dim(allowed, first_row, share)
    total = combine(
        (summit_share, mass_share, acc_share),
        tree_state(query_share, new_keys, new_values, allowed_share),
    )
    attention_share = (total[2] / total[1][..., None]).reshape(share, -1).astype(jnp.bfloat16)
    attention = lax.all_gather(attention_share, "seq", axis=0, tiled=True)
    partial_value = jnp.dot(attention, w_out, preferred_element_type=jnp.float32)
    return lax.psum_scatter(partial_value, "head", scatter_dimension=1, tiled=True).astype(
        jnp.bfloat16
    )


def solution(mesh):
    placed = (
        P("rep", "seq"),
        P("seq", "head"),
        P("seq", "head"),
        P("seq", "head"),
        P("head", "seq"),
        P("rep", "seq", "head"),
        P("rep", "seq", "head"),
        P("rep", None),
        P("rep"),
    )
    return jax.shard_map(
        local, mesh=mesh, in_specs=placed, out_specs=P("rep", ("seq", "head")), check_vma=False
    )
```

profile of v0, /device:TPU:0, one launch (start us, length us, event | category | flops | bytes accessed | tf_op | source)
XLA Modules:
  0.0 412.9 jit_solution(16273453118756324011)
XLA Ops:
  6.5 1.0 copy-done
  7.6 1.2 convolution_bitcast_fusion.1
  8.8 0.9 copy.84
  9.7 3.5 convolution_bitcast_fusion
  13.2 2.7 copy.76
  16.0 1.1 copy-done.6
  17.3 0.6 fusion.66
  18.0 1.0 copy.74
  19.2 1.0 copy.72
  20.4 1.8 fusion.47
  22.2 0.4 convolution_minimum_fusion.6
  22.6 0.3 convolution_minimum_fusion.5
  23.7 0.3 convolution_minimum_fusion.1
  24.0 0.4 fusion.67
  24.4 0.5 multiply_cosine_fusion
  25.0 110.8 %all-reduce.4.cloned.1.call-done = (f32[256,4,128]{2,0,1:T(8,128)}, f32[256,32,128]{2,1,0:T(8,128)}) async-done(((f32[256,4,128]{2,0,1:T(8,128)}, f32[256,32,128]{2,1,0:T(8,128)}), (f32[256,4,128]{2,0,1:T(8,128)}, f32[256,32,128]{2,1,0:T(8,128)})) %all-reduce.4.cloned.1.call-update) | async-done | bytes 4718608 | tf_op jit(solution)/shard_map/psum | solution.py:119
  135.7 4.8 %multiply_subtract_fusion = (bf16[256,32,64]{2,1,0:T(8,128)(2,1)S(1)}, bf16[256,32,64]{2,1,0:T(8,128)(2,1)S(1)}) fusion(f32[256,32,128]{2,1,0:T(8,128)} %get-tuple-element.40, f32[256,64]{1,0:T(8,128)S(1)} %get-tuple-element.81, f32[256,64]{1,0:T(8,128)S(1)} %get-tuple-element.80), kind=kLoop, calls=%fused_computation.17 | loop fusion | flops 4194304 | bytes 6422528 | tf_op jit(solution)/shard_map/sub | solution.py:35
  140.6 1.2 maximum_convert_fusion
  141.8 0.4 fusion.63
  142.1 0.4 copy.40
  142.5 1.3 bitcast_reduce_fusion
  143.9 3.1 fusion.6
  147.1 0.6 fusion.60
  147.7 0.4 copy.35
  148.1 1.3 bitcast_reduce_fusion.1
  149.5 2.4 fusion.4
  151.9 0.8 copy-done.3
  152.7 0.6 fusion.59
  153.3 60.0 %pmax.7 = f32[256,4,8]{0,2,1:T(8,128)S(1)} all-reduce(f32[256,4,8]{0,2,1:T(8,128)S(1)} %pad_maximum_fusion), channel_id=1, replica_groups=mesh['rep'=1,'seq'=16,'head'=2] {'seq'}, use_global_device_ids=true, to_apply=%region_4.5 | all-reduce | flops 8192 | bytes 65536 | tf_op jit(solution)/shard_map/pmax | solution.py:139
  213.3 0.6 fusion.43
  213.9 0.8 copy.69
  215.0 5.7 %bitcast_add_fusion = f32[128,4,8,128]{3,0,2,1:T(8,128)S(1)} fusion(bf16[512,4,128,1]{0,2,3,1:T(8,128)(2,1)S(1)} %bitcast.140, f32[4,128,8,512]{3,1,2,0:T(8,128)} %copy-done.2, f32[128,4,8]{0,2,1:T(8,128)S(1)} %broadcast_maximum_fusion, pred[512]{0:T(512)(128)(4,1)} %copy-done.19, f32[128,4,8]{0,2,1:T(8,128)} %get-tuple-element.79), kind=kOutput, calls=%fused_computation.25 | convolution fusion | flops 547880960 | bytes 11043328 | tf_op jit(solution)/shard_map/while/body/eval_jaxpr/rkgn,nkd->rkgd/dot_general | solution.py:71
  220.7 5.5 %bitcast_add_fusion.1 = f32[128,4,8,128]{3,0,2,1:T(8,128)S(1)} fusion(bf16[512,4,128,1]{0,2,3,1:T(8,128)(2,1)S(1)} %bitcast.139, f32[4,128,8,512]{3,1,2,0:T(8,128)} %copy-done.3, f32[128,4,8]{0,2,1:T(8,128)S(1)} %copy-done.11, pred[512]{0:T(512)(128)(4,1)S(1)} %copy-done.18, f32[128,4,8]{0,2,1:T(8,128)S(1)} %copy-done.16), kind=kOutput, calls=%fused_computation.26 | convolution fusion | flops 547880960 | bytes 11043328 | tf_op jit(solution)/shard_map/while/body/eval_jaxpr/rkgn,nkd->rkgd/dot_general | solution.py:71
  226.2 2.6 maximum_multiply_fusion
  229.2 0.6 copy-done.4
  229.8 2.1 fusion.69
  231.9 63.7 %all-reduce.5 = bf16[256,512]{1,0:T(8,128)(2,1)S(1)} all-reduce(f32[256,512]{1,0:T(8,128)} %fusion.69), channel_id=1, replica_groups=mesh['rep'=1,'seq'=16,'head'=2] {'seq'}, use_global_device_ids=true, to_apply=%region_8.9 | all-reduce | flops 131072 | bytes 786432 | tf_op jit(solution)/shard_map/psum | solution.py:119
  295.6 0.8 reshape.143
  296.4 0.8 copy.46
  297.5 0.4 fusion.68
  298.2 0.8 copy.70
  299.1 44.5 %reduce-scatter.6.cloned.1.call-done = f32[16,4,8,128]{3,0,2,1:T(8,128)} async-done(((f32[256,4,8,128]{3,0,2,1:T(8,128)}), f32[16,4,8,128]{3,0,2,1:T(8,128)}) %reduce-scatter.6.cloned.1.call-update) | async-done | bytes 262160 | tf_op jit(solution)/shard_map/reduce_scatter | solution.py:143
  343.5 1.4 fusion.25
  344.9 0.7 copy.86
  345.7 40.6 %all-gather.2.cloned.1.call-done = bf16[256,4096]{1,0:T(8,128)(2,1)} async-done(((bf16[16,4096]{1,0:T(8,128)(2,1)}), bf16[256,4096]{1,0:T(8,128)(2,1)}) %all-gather.2.cloned.1.call-update) | async-done | bytes 2097168 | tf_op jit(solution)/shard_map/all_gather | solution.py:155
  386.4 4.9 %fusion.70 = f32[256,512]{1,0:T(8,128)} fusion(bf16[256,4096]{1,0:T(8,128)(2,1)} %all-gather.2.cloned.1.call-done, bf16[4096,512]{1,0:T(8,128)(2,1)} %param.13), kind=kOutput, calls=%fused_computation.111 | convolution fusion | flops 1073741824 | bytes 6815744 | tf_op jit(solution)/shard_map/dot_general | solution.py:156
  391.3 13.5 %reduce-scatter.8.cloned.1.call-done = f32[256,256]{1,0:T(8,128)} async-done(((f32[256,512]{1,0:T(8,128)}), f32[256,256]{1,0:T(8,128)}) %reduce-scatter.8.cloned.1.call-update) | async-done | bytes 262160 | tf_op jit(solution)/shard_map/reduce_scatter | solution.py:157
  404.8 1.6 convert_element_type.65
  (73 shorter events, 3.0 us)
Async XLA Ops:
  6.5 1.0 copy-start
  6.5 129.2 %all-reduce.4.cloned.1.call-start = ((), (), s32[]{:S(2)}) async-start(), calls=%async_computation.7 | async-start | bytes 9437184 | tf_op jit(solution)/shard_map/psum | solution.py:119
  16.0 1.2 copy-start.6
  16.0 1.3 copy-start.20
  16.0 1.9 copy-start.7
  16.0 6.2 %copy-start.21 = (s32[2,128]{1,0:T(2,128)S(1)}, s32[2,128]{1,0:T(2,128)}, u32[]{:S(2)}) copy-start(s32[2,128]{1,0:T(2,128)} %param.16) | copy-start | bytes 3076
  16.0 282.2 %reduce-scatter.10.cloned.1.call-start = ((), (), s32[]{:S(2)}) async-start(), calls=%async_computation.6 | async-start | bytes 139264
  22.2 120.3 %copy-start.19 = (pred[512]{0:T(512)(128)(4,1)}, pred[512]{0:T(512)(128)(4,1)S(1)}, u32[]{:S(2)}) copy-start(pred[512]{0:T(512)(128)(4,1)S(1)} %get-tuple-element.92) | copy-start | bytes 1540
  143.9 3.2 copy-start.2
  143.9 4.3 %copy-start.17 = (pred[512]{0:T(512)(128)(4,1)S(1)}, pred[512]{0:T(512)(128)(4,1)}, u32[]{:S(2)}) copy-start(pred[512]{0:T(512)(128)(4,1)} %get-tuple-element.93) | copy-start | bytes 1540
  149.5 3.2 copy-start.3
  149.5 63.8 %copy-start.10 = (f32[128,4,8]{0,2,1:T(8,128)}, f32[128,4,8]{0,2,1:T(8,128)S(1)}, u32[]{:S(2)}) copy-start(f32[128,4,8]{0,2,1:T(8,128)S(1)} %broadcast_maximum_fusion.1) | copy-start | bytes 49156
  149.5 63.8 %copy-start.15 = (f32[128,4,8]{0,2,1:T(8,128)S(1)}, f32[128,4,8]{0,2,1:T(8,128)}, u32[]{:S(2)}) copy-start(f32[128,4,8]{0,2,1:T(8,128)} %get-tuple-element.78) | copy-start | bytes 49156
  149.5 65.4 %copy-start.9 = (bf16[1,512,512]{1,2,0:T(8,128)(2,1)S(1)}, bf16[1,512,512]{1,2,0:T(8,128)(2,1)}, u32[]{:S(2)}) copy-start(bf16[1,512,512]{1,2,0:T(8,128)(2,1)} %copy.74) | copy-start | bytes 1572868
  213.3 1.6 copy-start.12
  214.7 128.8 %reduce-scatter.6.cloned.1.call-start = ((), (), s32[]{:S(2)}) async-start(), calls=%async_computation.3 | async-start | bytes 4456448 | tf_op jit(solution)/shard_map/reduce_scatter | solution.py:143
  214.9 5.7 %copy-start.8 = (bf16[1,512,512]{1,2,0:T(8,128)(2,1)S(1)}, bf16[1,512,512]{1,2,0:T(8,128)(2,1)}, u32[]{:S(2)}) copy-start(bf16[1,512,512]{1,2,0:T(8,128)(2,1)} %copy.72) | copy-start | bytes 1572868
  215.0 5.7 %copy-start.11 = (f32[128,4,8]{0,2,1:T(8,128)S(1)}, f32[128,4,8]{0,2,1:T(8,128)}, u32[]{:S(2)}) copy-start(f32[128,4,8]{0,2,1:T(8,128)} %copy-done.10) | copy-start | bytes 49156
  215.0 5.7 %copy-start.16 = (f32[128,4,8]{0,2,1:T(8,128)S(1)}, f32[128,4,8]{0,2,1:T(8,128)}, u32[]{:S(2)}) copy-start(f32[128,4,8]{0,2,1:T(8,128)} %get-tuple-element.77) | copy-start | bytes 49156
  215.0 5.7 %copy-start.18 = (pred[512]{0:T(512)(128)(4,1)S(1)}, pred[512]{0:T(512)(128)(4,1)}, u32[]{:S(2)}) copy-start(pred[512]{0:T(512)(128)(4,1)} %get-tuple-element.93) | copy-start | bytes 1540
  220.7 5.5 %copy-start.14 = (f32[256,4,8]{0,2,1:T(8,128)S(1)}, f32[256,4,8]{0,2,1:T(8,128)}, u32[]{:S(2)}) copy-start(f32[256,4,8]{0,2,1:T(8,128)} %get-tuple-element.54) | copy-start | bytes 98308
  228.8 1.0 copy-start.4
  228.8 68.4 %copy-start.5 = (f32[256,4,128]{2,0,1:T(8,128)S(1)}, f32[256,4,128]{2,0,1:T(8,128)}, u32[]{:S(2)}) copy-start(f32[256,4,128]{2,0,1:T(8,128)} %get-tuple-element.39) | copy-start | bytes 1572868
  228.8 157.5 %all-gather.2.cloned.1.call-start = ((), (), s32[]{:S(2)}) async-start(), calls=%async_computation.4 | async-start | bytes 2228224 | tf_op jit(solution)/shard_map/all_gather | solution.py:155
  295.6 3.3 copy-start.13
  345.7 60.7 %copy-start.1 = (bf16[512,512]{1,0:T(8,128)(2,1)S(1)}, bf16[512,512]{1,0:T(8,128)(2,1)}, u32[]{:S(2)}) copy-start(bf16[512,512]{1,0:T(8,128)(2,1)} %param.11) | copy-start | bytes 1572868
  345.7 59.1 %reduce-scatter.8.cloned.1.call-start = ((), (), s32[]{:S(2)}) async-start(), calls=%async_computation.5 | async-start | bytes 786432 | tf_op jit(solution)/shard_map/reduce_scatter | solution.py:157
Sparse Core Ops, SparseCore 0:
  16.1 119.5 all-reduce.3
  214.8 52.9 reduce-scatter.9
  271.7 71.8 reduce-scatter.5
  345.8 40.5 all-gather.1
  391.4 13.3 reduce-scatter.7
where the time goes:
time: 414 us; the launch traced here: 413 us
  waiting for transfers between devices  209 us (50%)
  blocking collectives  124 us (30%)
  matrix products  29.4 us (7%)
  other arithmetic  20.9 us (5%)
  local copies, waits for them, and re-layouts  15.5 us (4%)
  between operations  13.6 us (3%)
    psum x1, waiting for transfers between devices, local(): q_raw, k_raw, v_raw = lax.psum((q_part, k_part, v_part), 'seq')  111 us
    psum x1, blocking collectives, local(): q_raw, k_raw, v_raw = lax.psum((q_part, k_part, v_part), 'seq')  63.7 us
    pmax x1, blocking collectives, local(): summit = lax.pmax(peak, 'seq')  60 us
    reduce_scatter x1, waiting for transfers between devices, local(): lax.psum_scatter(acc * factor[..., None], 'seq', scatter_dimension=0, til...  44.5 us
    all_gather x1, waiting for transfers between devices, local(): attention = lax.all_gather(attention_share, 'seq', axis=0, tiled=True)  40.6 us
    reduce_scatter x1, waiting for transfers between devices, local(): lax.psum_scatter(partial_value, 'head', scatter_dimension=1, tiled=True)  13.5 us
    unnamed x53, local copies, waits for them, and re-layouts  11.1 us
    dot_general x2, matrix products, step(): jnp.einsum('rkgn,nkd->rkgd', weights.astype(jnp.bfloat16), value_block, p...  11.1 us
  transfers between devices with their start and end apart: 5, of which 4 were waited for; matrix products, arithmetic and copies ran while one was open for 7% of the time, Pallas kernels for 0%

commit v1 on v0

--- a/solution.py
+++ b/solution.py
@@ -6,6 +6,12 @@
 HEAD_DIM = 128
 rope_base = 500000.0
 neg_big = -1e30
+
+
+def laid_out(blocks, dim):
+    blocks = jnp.moveaxis(blocks, 0, dim)
+    dims = blocks.shape
+    return blocks.reshape(*dims[:dim], dims[dim] * dims[dim + 1], *dims[dim + 2 :])
 
 
 def ancestry(parents):
@@ -152,7 +158,14 @@
         tree_state(query_share, new_keys, new_values, allowed_share),
     )
     attention_share = (total[2] / total[1][..., None]).reshape(share, -1).astype(jnp.bfloat16)
-    attention = lax.all_gather(attention_share, "seq", axis=0, tiled=True)
+    length_2 = lax.axis_size("seq")
+    forward = [(i, (i + 1) % length_2) for i in range(length_2)]
+    blocks = [attention_share]
+    while len(blocks) < length_2:
+        blocks.append(lax.ppermute(blocks[-1], "seq", forward))
+    index = lax.axis_index("seq")
+    blocks = jnp.stack(blocks)[(index - jnp.arange(length_2)) % length_2]
+    attention = laid_out(blocks, 0)
     partial_value = jnp.dot(attention, w_out, preferred_element_type=jnp.float32)
     return lax.psum_scatter(partial_value, "head", scatter_dimension=1, tiled=True).astype(
         jnp.bfloat16

time: 414 us -> 479 us (1.16)
  waiting for transfers between devices: 209 us -> 274 us
    ppermute x0 -> x15, waiting for transfers between devices: none -> 106 us  [local(): blocks.append(lax.ppermute(blocks[-1], 'seq', forward))]
    all_gather x1 -> x0, waiting for transfers between devices: 40.6 us -> none  [local(): attention = lax.all_gather(attention_share, 'seq', axis=0, tiled=True)]
    unnamed x53 -> x62, local copies, waits for them, and re-layouts: 11.1 us -> 11.5 us
  transfers between devices with their start and end apart: 5 -> 19, of which waited for: 4 -> 18; matrix products, arithmetic and copies ran while one was open for 7% -> 6% of each run, Pallas kernels for 0% -> 0%
where the time goes in v1:
time: 479 us; the launch traced here: 478 us
  waiting for transfers between devices  274 us (57%)
  blocking collectives  123 us (26%)
  matrix products  28.6 us (6%)
  other arithmetic  20.4 us (4%)
  local copies, waits for them, and re-layouts  18 us (4%)
  between operations  13.7 us (3%)
    psum x1, waiting for transfers between devices, local(): q_raw, k_raw, v_raw = lax.psum((q_part, k_part, v_part), 'seq')  111 us
    ppermute x15, waiting for transfers between devices, local(): blocks.append(lax.ppermute(blocks[-1], 'seq', forward))  106 us
    psum x1, blocking collectives, local(): q_raw, k_raw, v_raw = lax.psum((q_part, k_part, v_part), 'seq')  63.1 us
    pmax x1, blocking collectives, local(): summit = lax.pmax(peak, 'seq')  60 us
    reduce_scatter x1, waiting for transfers between devices, local(): lax.psum_scatter(acc * factor[..., None], 'seq', scatter_dimension=0, til...  45.1 us
    reduce_scatter x1, waiting for transfers between devices, local(): lax.psum_scatter(partial_value, 'head', scatter_dimension=1, tiled=True)  12 us
    unnamed x62, local copies, waits for them, and re-layouts  11.5 us
    dot_general x2, matrix products, step(): jnp.einsum('rkgn,nkd->rkgd', weights.astype(jnp.bfloat16), value_block, p...  11.2 us
  transfers between devices with their start and end apart: 19, of which 18 were waited for; matrix products, arithmetic and copies ran while one was open for 6% of the time, Pallas kernels for 0%

profile of v1, /device:TPU:0, one launch (start us, length us, event | category | flops | bytes accessed | tf_op | source)
XLA Modules:
  0.0 478.2 jit_solution(2876978829322091860)
XLA Ops:
  6.5 1.0 copy-done
  7.6 1.2 convolution_bitcast_fusion.1
  8.8 0.9 copy.86
  9.7 3.5 convolution_bitcast_fusion
  13.3 2.7 copy.78
  16.1 1.1 copy-done.7
  18.1 1.0 copy.76
  19.3 1.0 copy.74
  20.5 1.8 fusion.47
  25.1 110.7 %all-reduce.4.cloned.1.call-done = (f32[256,4,128]{2,0,1:T(8,128)}, f32[256,32,128]{2,1,0:T(8,128)}) async-done(((f32[256,4,128]{2,0,1:T(8,128)}, f32[256,32,128]{2,1,0:T(8,128)}), (f32[256,4,128]{2,0,1:T(8,128)}, f32[256,32,128]{2,1,0:T(8,128)})) %all-reduce.4.cloned.1.call-update) | async-done | bytes 4718608 | tf_op jit(solution)/shard_map/psum | solution.py:125
  135.8 4.9 %multiply_subtract_fusion = (bf16[256,32,64]{2,1,0:T(8,128)(2,1)S(1)}, bf16[256,32,64]{2,1,0:T(8,128)(2,1)S(1)}) fusion(f32[256,32,128]{2,1,0:T(8,128)} %get-tuple-element.40, f32[256,64]{1,0:T(8,128)S(1)} %get-tuple-element.81, f32[256,64]{1,0:T(8,128)S(1)} %get-tuple-element.80), kind=kLoop, calls=%fused_computation.18 | loop fusion | flops 4194304 | bytes 6422528 | tf_op jit(solution)/shard_map/sub | solution.py:41
  140.7 1.2 maximum_convert_fusion
  142.7 1.3 bitcast_reduce_fusion
  144.0 2.4 fusion.6
  146.4 0.8 copy-done.2
  148.3 1.3 bitcast_reduce_fusion.1
  149.6 2.4 fusion.4
  152.0 0.8 copy-done.3
  153.4 60.0 %pmax.7 = f32[256,4,8]{0,2,1:T(8,128)S(1)} all-reduce(f32[256,4,8]{0,2,1:T(8,128)S(1)} %pad_maximum_fusion), channel_id=1, replica_groups=mesh['rep'=1,'seq'=16,'head'=2] {'seq'}, use_global_device_ids=true, to_apply=%region_4.5 | all-reduce | flops 8192 | bytes 65536 | tf_op jit(solution)/shard_map/pmax | solution.py:145
  214.5 5.7 %bitcast_add_fusion = f32[128,4,8,128]{3,0,2,1:T(8,128)S(1)} fusion(bf16[512,4,128,1]{0,2,3,1:T(8,128)(2,1)S(1)} %bitcast.177, f32[4,128,8,512]{3,1,2,0:T(8,128)} %copy-done.2, f32[128,4,8]{0,2,1:T(8,128)S(1)} %broadcast_maximum_fusion, pred[512]{0:T(512)(128)(4,1)} %copy-done.16, f32[128,4,8]{0,2,1:T(8,128)} %get-tuple-element.79), kind=kOutput, calls=%fused_computation.26 | convolution fusion | flops 547880960 | bytes 11043328 | tf_op jit(solution)/shard_map/while/body/eval_jaxpr/rkgn,nkd->rkgd/dot_general | solution.py:77
  220.3 5.5 %bitcast_add_fusion.1 = f32[128,4,8,128]{3,0,2,1:T(8,128)S(1)} fusion(bf16[512,4,128,1]{0,2,3,1:T(8,128)(2,1)S(1)} %bitcast.176, f32[4,128,8,512]{3,1,2,0:T(8,128)} %copy-done.3, f32[128,4,8]{0,2,1:T(8,128)S(1)} %broadcast_maximum_fusion.1, pred[512]{0:T(512)(128)(4,1)S(1)} %copy-done.15, f32[128,4,8]{0,2,1:T(8,128)S(1)} %copy-done.13), kind=kOutput, calls=%fused_computation.27 | convolution fusion | flops 547880960 | bytes 11043328 | tf_op jit(solution)/shard_map/while/body/eval_jaxpr/rkgn,nkd->rkgd/dot_general | solution.py:77
  225.7 2.6 maximum_multiply_fusion
  229.3 1.3 fusion.71
  230.7 63.1 %all-reduce.5 = bf16[256,512]{1,0:T(8,128)(2,1)S(1)} all-reduce(f32[256,512]{1,0:T(8,128)S(1)} %fusion.71), channel_id=1, replica_groups=mesh['rep'=1,'seq'=16,'head'=2] {'seq'}, use_global_device_ids=true, to_apply=%region_8.9 | all-reduce | flops 131072 | bytes 786432 | tf_op jit(solution)/shard_map/psum | solution.py:125
  294.6 0.8 copy.47
  295.4 1.1 subtract_convert_fusion
  297.2 0.8 copy.72
  298.1 45.1 %reduce-scatter.6.cloned.1.call-done = f32[16,4,8,128]{3,0,2,1:T(8,128)} async-done(((f32[256,4,8,128]{3,0,2,1:T(8,128)}), f32[16,4,8,128]{3,0,2,1:T(8,128)}) %reduce-scatter.6.cloned.1.call-update) | async-done | bytes 262160 | tf_op jit(solution)/shard_map/reduce_scatter | solution.py:149
  343.2 1.3 fusion.25
  344.8 7.1 %collective-permute-done = bf16[16,4096]{1,0:T(8,128)(2,1)S(1)} collective-permute-done((bf16[16,4096]{1,0:T(8,128)(2,1)S(1)}, bf16[16,4096]{1,0:T(8,128)(2,1)S(1)}, u32[]{:S(2)}, u32[]{:S(2)}) %collective-permute-start) | collective-permute-done | bytes 131104 | tf_op jit(solution)/shard_map/ppermute | solution.py:165
  351.8 7.1 %collective-permute-done.1 = bf16[16,4096]{1,0:T(8,128)(2,1)S(1)} collective-permute-done((bf16[16,4096]{1,0:T(8,128)(2,1)S(1)}, bf16[16,4096]{1,0:T(8,128)(2,1)S(1)}, u32[]{:S(2)}, u32[]{:S(2)}) %collective-permute-start.1) | collective-permute-done | bytes 131104 | tf_op jit(solution)/shard_map/ppermute | solution.py:165
  358.9 7.1 %collective-permute-done.2 = bf16[16,4096]{1,0:T(8,128)(2,1)S(1)} collective-permute-done((bf16[16,4096]{1,0:T(8,128)(2,1)S(1)}, bf16[16,4096]{1,0:T(8,128)(2,1)S(1)}, u32[]{:S(2)}, u32[]{:S(2)}) %collective-permute-start.2) | collective-permute-done | bytes 131104 | tf_op jit(solution)/shard_map/ppermute | solution.py:165
  366.0 7.1 %collective-permute-done.3 = bf16[16,4096]{1,0:T(8,128)(2,1)S(1)} collective-permute-done((bf16[16,4096]{1,0:T(8,128)(2,1)S(1)}, bf16[16,4096]{1,0:T(8,128)(2,1)S(1)}, u32[]{:S(2)}, u32[]{:S(2)}) %collective-permute-start.3) | collective-permute-done | bytes 131104 | tf_op jit(solution)/shard_map/ppermute | solution.py:165
  373.1 7.1 %collective-permute-done.4 = bf16[16,4096]{1,0:T(8,128)(2,1)S(1)} collective-permute-done((bf16[16,4096]{1,0:T(8,128)(2,1)S(1)}, bf16[16,4096]{1,0:T(8,128)(2,1)S(1)}, u32[]{:S(2)}, u32[]{:S(2)}) %collective-permute-start.4) | collective-permute-done | bytes 131104 | tf_op jit(solution)/shard_map/ppermute | solution.py:165
  380.2 7.1 %collective-permute-done.5 = bf16[16,4096]{1,0:T(8,128)(2,1)S(1)} collective-permute-done((bf16[16,4096]{1,0:T(8,128)(2,1)S(1)}, bf16[16,4096]{1,0:T(8,128)(2,1)S(1)}, u32[]{:S(2)}, u32[]{:S(2)}) %collective-permute-start.5) | collective-permute-done | bytes 131104 | tf_op jit(solution)/shard_map/ppermute | solution.py:165
  387.3 7.1 %collective-permute-done.6 = bf16[16,4096]{1,0:T(8,128)(2,1)S(1)} collective-permute-done((bf16[16,4096]{1,0:T(8,128)(2,1)S(1)}, bf16[16,4096]{1,0:T(8,128)(2,1)S(1)}, u32[]{:S(2)}, u32[]{:S(2)}) %collective-permute-start.6) | collective-permute-done | bytes 131104 | tf_op jit(solution)/shard_map/ppermute | solution.py:165
  394.4 7.1 %collective-permute-done.7 = bf16[16,4096]{1,0:T(8,128)(2,1)S(1)} collective-permute-done((bf16[16,4096]{1,0:T(8,128)(2,1)S(1)}, bf16[16,4096]{1,0:T(8,128)(2,1)S(1)}, u32[]{:S(2)}, u32[]{:S(2)}) %collective-permute-start.7) | collective-permute-done | bytes 131104 | tf_op jit(solution)/shard_map/ppermute | solution.py:165
  401.5 7.1 %collective-permute-done.8 = bf16[16,4096]{1,0:T(8,128)(2,1)S(1)} collective-permute-done((bf16[16,4096]{1,0:T(8,128)(2,1)S(1)}, bf16[16,4096]{1,0:T(8,128)(2,1)S(1)}, u32[]{:S(2)}, u32[]{:S(2)}) %collective-permute-start.8) | collective-permute-done | bytes 131104 | tf_op jit(solution)/shard_map/ppermute | solution.py:165
  408.6 7.1 %collective-permute-done.9 = bf16[16,4096]{1,0:T(8,128)(2,1)S(1)} collective-permute-done((bf16[16,4096]{1,0:T(8,128)(2,1)S(1)}, bf16[16,4096]{1,0:T(8,128)(2,1)S(1)}, u32[]{:S(2)}, u32[]{:S(2)}) %collective-permute-start.9) | collective-permute-done | bytes 131104 | tf_op jit(solution)/shard_map/ppermute | solution.py:165
  415.6 7.1 %collective-permute-done.10 = bf16[16,4096]{1,0:T(8,128)(2,1)S(1)} collective-permute-done((bf16[16,4096]{1,0:T(8,128)(2,1)S(1)}, bf16[16,4096]{1,0:T(8,128)(2,1)S(1)}, u32[]{:S(2)}, u32[]{:S(2)}) %collective-permute-start.10) | collective-permute-done | bytes 131104 | tf_op jit(solution)/shard_map/ppermute | solution.py:165
  422.7 7.1 %collective-permute-done.11 = bf16[16,4096]{1,0:T(8,128)(2,1)S(1)} collective-permute-done((bf16[16,4096]{1,0:T(8,128)(2,1)S(1)}, bf16[16,4096]{1,0:T(8,128)(2,1)S(1)}, u32[]{:S(2)}, u32[]{:S(2)}) %collective-permute-start.11) | collective-permute-done | bytes 131104 | tf_op jit(solution)/shard_map/ppermute | solution.py:165
  429.8 7.1 %collective-permute-done.12 = bf16[16,4096]{1,0:T(8,128)(2,1)S(1)} collective-permute-done((bf16[16,4096]{1,0:T(8,128)(2,1)S(1)}, bf16[16,4096]{1,0:T(8,128)(2,1)S(1)}, u32[]{:S(2)}, u32[]{:S(2)}) %collective-permute-start.12) | collective-permute-done | bytes 131104 | tf_op jit(solution)/shard_map/ppermute | solution.py:165
  436.9 7.1 %collective-permute-done.13 = bf16[16,4096]{1,0:T(8,128)(2,1)S(1)} collective-permute-done((bf16[16,4096]{1,0:T(8,128)(2,1)S(1)}, bf16[16,4096]{1,0:T(8,128)(2,1)S(1)}, u32[]{:S(2)}, u32[]{:S(2)}) %collective-permute-start.13) | collective-permute-done | bytes 131104 | tf_op jit(solution)/shard_map/ppermute | solution.py:165
  444.0 7.1 %collective-permute-done.14 = bf16[16,4096]{1,0:T(8,128)(2,1)S(1)} collective-permute-done((bf16[16,4096]{1,0:T(8,128)(2,1)S(1)}, bf16[16,4096]{1,0:T(8,128)(2,1)S(1)}, u32[]{:S(2)}, u32[]{:S(2)}) %collective-permute-start.14) | collective-permute-done | bytes 131104 | tf_op jit(solution)/shard_map/ppermute | solution.py:165
  451.1 2.0 gather_fusion
  453.1 4.9 %fusion.72 = f32[256,512]{1,0:T(8,128)} fusion(bf16[256,4096]{1,0:T(8,128)(2,1)} %bitcast.174, bf16[4096,512]{1,0:T(8,128)(2,1)} %param.13), kind=kOutput, calls=%fused_computation.135 | convolution fusion | flops 1073741824 | bytes 6815744 | tf_op jit(solution)/shard_map/dot_general | solution.py:169
  458.0 12.0 %reduce-scatter.8.cloned.1.call-done = f32[256,256]{1,0:T(8,128)} async-done(((f32[256,512]{1,0:T(8,128)}), f32[256,256]{1,0:T(8,128)}) %reduce-scatter.8.cloned.1.call-update) | async-done | bytes 262160 | tf_op jit(solution)/shard_map/reduce_scatter | solution.py:170
  470.1 1.6 convert_element_type.76
  (114 shorter events, 10.4 us)
Async XLA Ops:
  6.5 1.0 copy-start
  6.5 129.3 %all-reduce.4.cloned.1.call-start = ((), (), s32[]{:S(2)}) async-start(), calls=%async_computation.6 | async-start | bytes 9437184 | tf_op jit(solution)/shard_map/psum | solution.py:125
  16.0 1.2 copy-start.7
  16.0 1.3 copy-start.17
  16.0 2.0 copy-start.8
  16.0 6.3 %copy-start.18 = (s32[2,128]{1,0:T(2,128)S(1)}, s32[2,128]{1,0:T(2,128)}, u32[]{:S(2)}) copy-start(s32[2,128]{1,0:T(2,128)} %param.16) | copy-start | bytes 3076
  16.1 281.2 %reduce-scatter.10.cloned.1.call-start = ((), (), s32[]{:S(2)}) async-start(), calls=%async_computation.5 | async-start | bytes 139264
  22.3 121.7 %copy-start.16 = (pred[512]{0:T(512)(128)(4,1)}, pred[512]{0:T(512)(128)(4,1)S(1)}, u32[]{:S(2)}) copy-start(pred[512]{0:T(512)(128)(4,1)S(1)} %get-tuple-element.92) | copy-start | bytes 1540
  25.1 115.7 %copy-start.6 = (f32[256,64]{1,0:T(8,128)}, f32[256,64]{1,0:T(8,128)S(1)}, u32[]{:S(2)}) copy-start(f32[256,64]{1,0:T(8,128)S(1)} %get-tuple-element.81) | copy-start | bytes 196612
  144.0 3.2 copy-start.2
  144.0 4.2 copy-start.14
  149.6 3.3 copy-start.3
  149.6 64.8 %copy-start.10 = (bf16[1,512,512]{1,2,0:T(8,128)(2,1)S(1)}, bf16[1,512,512]{1,2,0:T(8,128)(2,1)}, u32[]{:S(2)}) copy-start(bf16[1,512,512]{1,2,0:T(8,128)(2,1)} %copy.76) | copy-start | bytes 1572868
  213.4 6.8 %copy-start.11 = (f32[256,4,8]{0,2,1:T(8,128)}, f32[256,4,8]{0,2,1:T(8,128)S(1)}, u32[]{:S(2)}) copy-start(f32[256,4,8]{0,2,1:T(8,128)S(1)} %pmax.7) | copy-start | bytes 98308
  214.2 129.0 %reduce-scatter.6.cloned.1.call-start = ((), (), s32[]{:S(2)}) async-start(), calls=%async_computation.3 | async-start | bytes 4456448 | tf_op jit(solution)/shard_map/reduce_scatter | solution.py:149
  214.4 5.8 %copy-start.9 = (bf16[1,512,512]{1,2,0:T(8,128)(2,1)S(1)}, bf16[1,512,512]{1,2,0:T(8,128)(2,1)}, u32[]{:S(2)}) copy-start(bf16[1,512,512]{1,2,0:T(8,128)(2,1)} %copy.74) | copy-start | bytes 1572868
  214.5 5.8 %copy-start.13 = (f32[128,4,8]{0,2,1:T(8,128)S(1)}, f32[128,4,8]{0,2,1:T(8,128)}, u32[]{:S(2)}) copy-start(f32[128,4,8]{0,2,1:T(8,128)} %get-tuple-element.77) | copy-start | bytes 49156
  214.5 5.8 %copy-start.15 = (pred[512]{0:T(512)(128)(4,1)S(1)}, pred[512]{0:T(512)(128)(4,1)}, u32[]{:S(2)}) copy-start(pred[512]{0:T(512)(128)(4,1)} %get-tuple-element.93) | copy-start | bytes 1540
  228.3 1.0 copy-start.4
  228.3 67.1 %copy-start.5 = (f32[256,4,128]{2,0,1:T(8,128)S(1)}, f32[256,4,128]{2,0,1:T(8,128)}, u32[]{:S(2)}) copy-start(f32[256,4,128]{2,0,1:T(8,128)} %get-tuple-element.39) | copy-start | bytes 1572868
  228.3 241.7 %reduce-scatter.8.cloned.1.call-start = ((), (), s32[]{:S(2)}) async-start(), calls=%async_computation.4 | async-start | bytes 786432 | tf_op jit(solution)/shard_map/reduce_scatter | solution.py:170
  293.8 4.2 copy-start.12
  344.7 7.1 %collective-permute-start = (bf16[16,4096]{1,0:T(8,128)(2,1)S(1)}, bf16[16,4096]{1,0:T(8,128)(2,1)S(1)}, u32[]{:S(2)}, u32[]{:S(2)}) collective-permute-start(bf16[16,4096]{1,0:T(8,128)(2,1)S(1)} %bitcast.180), channel_id=1, source_target_pairs={{0,2},{2,4},{4,6},{6,8},{8,10},{10,12},{12,14},{14,16},{16,18},{18... | collective-permute-start | bytes 393224 | tf_op jit(solution)/shard_map/ppermute | solution.py:165
  351.8 7.1 %collective-permute-start.1 = (bf16[16,4096]{1,0:T(8,128)(2,1)S(1)}, bf16[16,4096]{1,0:T(8,128)(2,1)S(1)}, u32[]{:S(2)}, u32[]{:S(2)}) collective-permute-start(bf16[16,4096]{1,0:T(8,128)(2,1)S(1)} %collective-permute-done), channel_id=1, source_target_pairs={{0,2},{2,4},{4,6},{6,8},{8,10},{10,12},{12,14},{14,16},{16,18},{18... | collective-permute-start | bytes 393224 | tf_op jit(solution)/shard_map/ppermute | solution.py:165
  358.9 7.1 %collective-permute-start.2 = (bf16[16,4096]{1,0:T(8,128)(2,1)S(1)}, bf16[16,4096]{1,0:T(8,128)(2,1)S(1)}, u32[]{:S(2)}, u32[]{:S(2)}) collective-permute-start(bf16[16,4096]{1,0:T(8,128)(2,1)S(1)} %collective-permute-done.1), channel_id=1, source_target_pairs={{0,2},{2,4},{4,6},{6,8},{8,10},{10,12},{12,14},{14,16},{16,18},{18... | collective-permute-start | bytes 393224 | tf_op jit(solution)/shard_map/ppermute | solution.py:165
  366.0 7.1 %collective-permute-start.3 = (bf16[16,4096]{1,0:T(8,128)(2,1)S(1)}, bf16[16,4096]{1,0:T(8,128)(2,1)S(1)}, u32[]{:S(2)}, u32[]{:S(2)}) collective-permute-start(bf16[16,4096]{1,0:T(8,128)(2,1)S(1)} %collective-permute-done.2), channel_id=1, source_target_pairs={{0,2},{2,4},{4,6},{6,8},{8,10},{10,12},{12,14},{14,16},{16,18},{18... | collective-permute-start | bytes 393224 | tf_op jit(solution)/shard_map/ppermute | solution.py:165
  373.1 7.1 %collective-permute-start.4 = (bf16[16,4096]{1,0:T(8,128)(2,1)S(1)}, bf16[16,4096]{1,0:T(8,128)(2,1)S(1)}, u32[]{:S(2)}, u32[]{:S(2)}) collective-permute-start(bf16[16,4096]{1,0:T(8,128)(2,1)S(1)} %collective-permute-done.3), channel_id=1, source_target_pairs={{0,2},{2,4},{4,6},{6,8},{8,10},{10,12},{12,14},{14,16},{16,18},{18... | collective-permute-start | bytes 393224 | tf_op jit(solution)/shard_map/ppermute | solution.py:165
  380.2 7.1 %collective-permute-start.5 = (bf16[16,4096]{1,0:T(8,128)(2,1)S(1)}, bf16[16,4096]{1,0:T(8,128)(2,1)S(1)}, u32[]{:S(2)}, u32[]{:S(2)}) collective-permute-start(bf16[16,4096]{1,0:T(8,128)(2,1)S(1)} %collective-permute-done.4), channel_id=1, source_target_pairs={{0,2},{2,4},{4,6},{6,8},{8,10},{10,12},{12,14},{14,16},{16,18},{18... | collective-permute-start | bytes 393224 | tf_op jit(solution)/shard_map/ppermute | solution.py:165
  387.3 7.1 %collective-permute-start.6 = (bf16[16,4096]{1,0:T(8,128)(2,1)S(1)}, bf16[16,4096]{1,0:T(8,128)(2,1)S(1)}, u32[]{:S(2)}, u32[]{:S(2)}) collective-permute-start(bf16[16,4096]{1,0:T(8,128)(2,1)S(1)} %collective-permute-done.5), channel_id=1, source_target_pairs={{0,2},{2,4},{4,6},{6,8},{8,10},{10,12},{12,14},{14,16},{16,18},{18... | collective-permute-start | bytes 393224 | tf_op jit(solution)/shard_map/ppermute | solution.py:165
  394.4 7.1 %collective-permute-start.7 = (bf16[16,4096]{1,0:T(8,128)(2,1)S(1)}, bf16[16,4096]{1,0:T(8,128)(2,1)S(1)}, u32[]{:S(2)}, u32[]{:S(2)}) collective-permute-start(bf16[16,4096]{1,0:T(8,128)(2,1)S(1)} %collective-permute-done.6), channel_id=1, source_target_pairs={{0,2},{2,4},{4,6},{6,8},{8,10},{10,12},{12,14},{14,16},{16,18},{18... | collective-permute-start | bytes 393224 | tf_op jit(solution)/shard_map/ppermute | solution.py:165
  401.4 7.1 %collective-permute-start.8 = (bf16[16,4096]{1,0:T(8,128)(2,1)S(1)}, bf16[16,4096]{1,0:T(8,128)(2,1)S(1)}, u32[]{:S(2)}, u32[]{:S(2)}) collective-permute-start(bf16[16,4096]{1,0:T(8,128)(2,1)S(1)} %collective-permute-done.7), channel_id=1, source_target_pairs={{0,2},{2,4},{4,6},{6,8},{8,10},{10,12},{12,14},{14,16},{16,18},{18... | collective-permute-start | bytes 393224 | tf_op jit(solution)/shard_map/ppermute | solution.py:165
  408.5 7.1 %collective-permute-start.9 = (bf16[16,4096]{1,0:T(8,128)(2,1)S(1)}, bf16[16,4096]{1,0:T(8,128)(2,1)S(1)}, u32[]{:S(2)}, u32[]{:S(2)}) collective-permute-start(bf16[16,4096]{1,0:T(8,128)(2,1)S(1)} %collective-permute-done.8), channel_id=1, source_target_pairs={{0,2},{2,4},{4,6},{6,8},{8,10},{10,12},{12,14},{14,16},{16,18},{18... | collective-permute-start | bytes 393224 | tf_op jit(solution)/shard_map/ppermute | solution.py:165
  415.6 7.1 %collective-permute-start.10 = (bf16[16,4096]{1,0:T(8,128)(2,1)S(1)}, bf16[16,4096]{1,0:T(8,128)(2,1)S(1)}, u32[]{:S(2)}, u32[]{:S(2)}) collective-permute-start(bf16[16,4096]{1,0:T(8,128)(2,1)S(1)} %collective-permute-done.9), channel_id=1, source_target_pairs={{0,2},{2,4},{4,6},{6,8},{8,10},{10,12},{12,14},{14,16},{16,18},{18... | collective-permute-start | bytes 393224 | tf_op jit(solution)/shard_map/ppermute | solution.py:165
  422.7 7.1 %collective-permute-start.11 = (bf16[16,4096]{1,0:T(8,128)(2,1)S(1)}, bf16[16,4096]{1,0:T(8,128)(2,1)S(1)}, u32[]{:S(2)}, u32[]{:S(2)}) collective-permute-start(bf16[16,4096]{1,0:T(8,128)(2,1)S(1)} %collective-permute-done.10), channel_id=1, source_target_pairs={{0,2},{2,4},{4,6},{6,8},{8,10},{10,12},{12,14},{14,16},{16,18},{18... | collective-permute-start | bytes 393224 | tf_op jit(solution)/shard_map/ppermute | solution.py:165
  429.8 7.1 %collective-permute-start.12 = (bf16[16,4096]{1,0:T(8,128)(2,1)S(1)}, bf16[16,4096]{1,0:T(8,128)(2,1)S(1)}, u32[]{:S(2)}, u32[]{:S(2)}) collective-permute-start(bf16[16,4096]{1,0:T(8,128)(2,1)S(1)} %collective-permute-done.11), channel_id=1, source_target_pairs={{0,2},{2,4},{4,6},{6,8},{8,10},{10,12},{12,14},{14,16},{16,18},{18... | collective-permute-start | bytes 393224 | tf_op jit(solution)/shard_map/ppermute | solution.py:165
  436.9 7.1 %collective-permute-start.13 = (bf16[16,4096]{1,0:T(8,128)(2,1)S(1)}, bf16[16,4096]{1,0:T(8,128)(2,1)S(1)}, u32[]{:S(2)}, u32[]{:S(2)}) collective-permute-start(bf16[16,4096]{1,0:T(8,128)(2,1)S(1)} %collective-permute-done.12), channel_id=1, source_target_pairs={{0,2},{2,4},{4,6},{6,8},{8,10},{10,12},{12,14},{14,16},{16,18},{18... | collective-permute-start | bytes 393224 | tf_op jit(solution)/shard_map/ppermute | solution.py:165
  444.0 7.1 %collective-permute-start.14 = (bf16[16,4096]{1,0:T(8,128)(2,1)S(1)}, bf16[16,4096]{1,0:T(8,128)(2,1)S(1)}, u32[]{:S(2)}, u32[]{:S(2)}) collective-permute-start(bf16[16,4096]{1,0:T(8,128)(2,1)S(1)} %collective-permute-done.13), channel_id=1, source_target_pairs={{0,2},{2,4},{4,6},{6,8},{8,10},{10,12},{12,14},{14,16},{16,18},{18... | collective-permute-start | bytes 393224 | tf_op jit(solution)/shard_map/ppermute | solution.py:165
  453.1 18.6 %copy-start.1 = (bf16[512,512]{1,0:T(8,128)(2,1)S(1)}, bf16[512,512]{1,0:T(8,128)(2,1)}, u32[]{:S(2)}) copy-start(bf16[512,512]{1,0:T(8,128)(2,1)} %param.11) | copy-start | bytes 1572868
Sparse Core Ops, SparseCore 0:
  16.2 119.5 all-reduce.3
  214.3 52.8 reduce-scatter.9
  271.1 72.0 reduce-scatter.5
  458.2 11.8 reduce-scatter.7
